TPU v7x, 128 devices: a whole 4x4x4 slice. The times are simulated.
128 devices in a mesh: rep: 4 (over x), ep: 32 (over y, z, core).
Axes of the slice: x: 4, y: 4, z: 4, core: 2. Of those that a mesh axis runs over, the one named last changes fastest.
Arguments:
- q_latent: bfloat16 [1024, 128, 512], P(('rep', 'ep')), may hold values from -6 to 6
- q_rope: bfloat16 [1024, 128, 64], P(('rep', 'ep')), may hold values from -104 to 104
- cache_latent: bfloat16 [1024, 128, 512], P(('rep', 'ep')), may hold values from -6 to 6
- cache_rope: bfloat16 [1024, 128, 64], P(('rep', 'ep')), may hold values from -6 to 6
- cache_len: int32 [1024], P(('rep', 'ep')), may hold values from 32 to 128, as said below
- stream: bfloat16 [1024, 7168], P(('rep', 'ep')), may hold values from -6 to 6
- norm_gain: float32 [7168], replicated, may hold values from 0.1 to 1.9
- expert_ids: int32 [1024, 8], P(('rep', 'ep')), may hold values from 0 to 63, all different within a row; in each aligned block of 8 rows (0 to 7, 8 to 15, ...) at most 2 rows name the same one
- route_weights: bfloat16 [1024, 8], P(('rep', 'ep')), may hold values from 0.099609375 to 1
- w_gate: bfloat16 [64, 7168, 1024], P('ep', None, 'rep'), may hold values from -0.0625 to 0.0625
- w_up: bfloat16 [64, 7168, 1024], P('ep', None, 'rep'), may hold values from -0.0625 to 0.0625
- w_down: bfloat16 [64, 1024, 7168], P('ep', 'rep'), may hold values from -0.1875 to 0.1875
Outputs:
- attn_latent: bfloat16 [1024, 128, 512], P(('rep', 'ep'))
- layer_out: bfloat16 [1024, 7168], P(('rep', 'ep'))
Inputs may be any that keep to these rules, and one draw needn't show every extreme that they name: `expert_ids`: each row names 8 different experts; within the rows of one device no expert is named by more than 2 rows, a bound that some block reaches. `cache_len`: some row has all 128 positions live.
All inputs are finite; a program needn't handle non-finite values.
Results may differ from a plain program's by a relative error of at most 0.01.
Values may be sent and summed in bfloat16 or wider, within the bound.
No kernel may reach another device: no remote copies, remote signals or barrier semaphores. Data moves between devices by JAX's collectives and lax.ppermute only.
A program may use at most 128 MiB of HBM per device.

v0:
```python
import jax
import jax.numpy as jnp
from jax import lax
from jax.sharding import Mesh
from jax.sharding import PartitionSpec as P

EP = ("ep_0", "ep_1", "ep_2")
REP_EP = ("rep", "ep_0", "ep_1", "ep_2")
score_scale = 192.0 ** (-0.5)
norm_eps = 1e-06


def cut_along(shard, dim, count):
    before, after = (shard.shape[:dim], shard.shape[dim + 1 :])
    return jnp.moveaxis(shard.reshape(*before, count, -1, *after), dim, 0)


def in_order(tiles, dim):
    tiles = jnp.moveaxis(tiles, 0, dim)
    dims = tiles.shape
    return tiles.reshape(*dims[:dim], dims[dim] * dims[dim + 1], *dims[dim + 2 :])


def moved_by_axis(tiles, axes, turns):
    inside = tiles.shape[1:]
    result = tiles.reshape(*(lax.axis_size(a) for a in axes), *inside)
    for k in turns:
        result = lax.all_to_all(result, axes[k], k, k, tiled=True)
    return result.reshape(-1, *inside)


def core_and_chips(shard, groups, turns, split_dim, concat_dim):
    count = lax.axis_size(groups[0]) * lax.axis_size(groups[1])
    tiles = cut_along(shard, split_dim, count)
    return in_order(moved_by_axis(tiles, groups, turns), concat_dim)


def slot_ranks(route_table, expert_total):
    onehot = (route_table[..., None] == jnp.arange(expert_total, dtype=jnp.int32)).astype(jnp.int32)
    earlier = jnp.cumsum(onehot, axis=1) - onehot
    return jnp.sum(earlier * onehot, axis=-1)


def fill_slots(features, slot_index, row_index, slot_total):
    sources = jnp.zeros((slot_total,), jnp.int32).at[slot_index].set(row_index)
    filled = jnp.zeros((slot_total,), features.dtype).at[slot_index].set(1)
    return features[sources] * filled[:, None]


def expert_block(tokens_in, gate_part, up_part, down_part):
    gate_act = jnp.dot(tokens_in, gate_part, preferred_element_type=jnp.float32)
    up_act = jnp.dot(tokens_in, up_part, preferred_element_type=jnp.float32)
    hidden = (jax.nn.silu(gate_act) * up_act).astype(jnp.bfloat16)
    return jnp.dot(hidden, down_part, preferred_element_type=jnp.float32).astype(jnp.bfloat16)


def per_device(
    q_latent,
    q_rope,
    cache_latent,
    cache_rope,
    cache_len,
    stream,
    norm_gain,
    expert_ids,
    route_weights,
    w_gate,
    w_up,
    w_down,
):
    ep_count = lax.axis_size(EP)
    row_count, feature_dim = stream.shape
    local_count = w_gate.shape[0]
    top_count = expert_ids.shape[1]
    expert_total = local_count * ep_count
    capacity = max(2, 2 * row_count * top_count // expert_total)
    stream_f = stream.astype(jnp.float32)
    normed = (
        stream_f
        * lax.rsqrt(jnp.mean(stream_f * stream_f, axis=-1, keepdims=True) + norm_eps)
        * norm_gain
    ).astype(jnp.bfloat16)
    flat_routes = expert_ids.reshape(-1)
    rank_in = slot_ranks(flat_routes.reshape(1, -1), expert_total)[0]
    expert_slot = flat_routes % local_count * ep_count + flat_routes // local_count
    slot_index = expert_slot * capacity + rank_in
    row_index = jnp.arange(row_count * top_count, dtype=jnp.int32) // top_count
    slot_total = expert_total * capacity
    outgoing = fill_slots(normed, slot_index, row_index, slot_total).reshape(
        local_count, ep_count, capacity, feature_dim
    )
    incoming = core_and_chips(outgoing, (("ep_0", "ep_1"), "ep_2"), (1, 0), 1, 1)
    incoming = incoming.reshape(local_count, ep_count * capacity, feature_dim)
    scores = (
        jnp.einsum("ihl,itl->iht", q_latent, cache_latent, preferred_element_type=jnp.float32)
        + jnp.einsum("ihr,itr->iht", q_rope, cache_rope, preferred_element_type=jnp.float32)
    ) * score_scale
    valid_mask = (
        jnp.arange(cache_latent.shape[1], dtype=jnp.int32)[None, None, :] < cache_len[:, None, None]
    )
    scores = jnp.where(valid_mask, scores, -1e30)
    top_score = jnp.max(scores, axis=-1, keepdims=True)
    exponent = jnp.where(valid_mask, jnp.exp(scores - top_score), 0.0)
    attn_weights = (exponent / jnp.sum(exponent, axis=-1, keepdims=True)).astype(jnp.bfloat16)
    attn_latent = jnp.einsum(
        "iht,itl->ihl", attn_weights, cache_latent, preferred_element_type=jnp.float32
    ).astype(jnp.bfloat16)
    everyone = lax.all_gather(incoming, "rep", axis=1, tiled=True)
    partials = jax.vmap(expert_block)(everyone, w_gate, w_up, w_down)
    partials = lax.optimization_barrier(partials)
    summed = lax.psum_scatter(
        partials.astype(jnp.float32).astype(jnp.bfloat16), "rep", scatter_dimension=1, tiled=True
    ).astype(jnp.float32)
    returned = lax.all_to_all(
        summed.reshape(local_count, ep_count, capacity, feature_dim).astype(jnp.bfloat16),
        EP,
        split_axis=1,
        concat_axis=1,
        tiled=True,
    ).astype(jnp.float32)
    picked = returned.reshape(slot_total, feature_dim)[slot_index].reshape(
        row_count, top_count, feature_dim
    )
    expert_sum = jnp.einsum(
        "rk,rkd->rd", route_weights.astype(jnp.float32), picked, precision=lax.Precision.HIGHEST
    )
    layer_out = (stream_f + expert_sum).astype(jnp.bfloat16)
    return (attn_latent, layer_out)


def solution(mesh):
    torus = Mesh(mesh.devices.reshape(mesh.shape["rep"], 4, 4, 2), ("rep", "ep_0", "ep_1", "ep_2"))
    return jax.shard_map(
        per_device,
        mesh=torus,
        in_specs=(
            P(REP_EP, None, None),
            P(REP_EP, None, None),
            P(REP_EP, None, None),
            P(REP_EP, None, None),
            P(REP_EP),
            P(REP_EP, None),
            P(),
            P(REP_EP, None),
            P(REP_EP, None),
            P(EP, None, "rep"),
            P(EP, None, "rep"),
            P(EP, "rep", None),
        ),
        out_specs=(P(REP_EP, None, None), P(REP_EP, None)),
        check_vma=False,
    )
```

profile of v0, /device:TPU:1, one launch (start us, length us, event | category | flops | bytes accessed | tf_op | source)
XLA Modules:
  0.0 291.7 jit_solution(6912116747219094064)
XLA Ops:
  7.2 0.0 copy-start
  7.2 0.0 all-gather.2.cloned.1.call-start
  7.2 0.8 eq.29
  8.1 0.8 reshape.284
  8.8 0.1 fusion.20
  8.9 0.1 reduce_window_sum.11
  9.0 0.2 select_reduce_fusion
  9.2 0.8 scatter_custom_fusion
  10.0 1.1 fusion.16
  11.1 1.0 fusion.18
  12.1 1.7 gather_fusion
  13.8 1.7 gather.9
  15.5 1.0 scatter_custom_fusion.1
  16.5 0.1 mul.87
  16.7 3.1 %copy_multiply_fusion = bf16[2,32,1,2,7168]{4,3,0,1,2:T(2,128)(2,1)S(1)} fusion(bf16[2,32,1,2,7168]{4,3,1,0,2:T(2,128)(2,1)} %gather.9, bf16[2,32,2]{2,0,1:T(2,128)(2,1)S(1)} %copy.21), kind=kLoop, calls=%fused_computation.6 | loop fusion | flops 917504 | bytes 3670272 | tf_op jit(solution)/shard_map/mul | solution.py:47
  19.8 1.3 copy.23
  21.1 6.2 %all_to_all.15 = bf16[16,2,2,1,2,7168]{5,4,0,2,3,1:T(2,128)(2,1)S(1)} all-to-all(bf16[16,2,2,1,2,7168]{5,4,0,2,3,1:T(2,128)(2,1)S(1)} %copy.23), channel_id=1, replica_groups=mesh['rep'=4,'ep_0'=4,'ep_1'=4,'ep_2'=2] {'ep_2'}, dimensions={1} | all-to-all | bytes 3670016 | tf_op jit(solution)/shard_map/all_to_all | solution.py:28
  27.3 1.7 copy.24
  29.0 32.2 %all_to_all.16 = bf16[16,2,2,1,2,7168]{5,4,1,2,3,0:T(2,128)(2,1)S(1)} all-to-all(bf16[16,2,2,1,2,7168]{5,4,1,2,3,0:T(2,128)(2,1)S(1)} %copy.24), channel_id=1, replica_groups=mesh['rep'=4,'ep_0'=4,'ep_1'=4,'ep_2'=2] {'ep_0','ep_1'}, dimensions={0} | all-to-all | bytes 3670016 | tf_op jit(solution)/shard_map/all_to_all | solution.py:28
  61.2 1.3 copy.25
  62.5 1.3 copy.26
  63.8 1.7 reshape_reshape.4
  65.5 0.0 all-gather.2.cloned.1.call-update
  65.6 0.2 reduce-scatter.2.cloned.1.call-start
  65.8 73.1 %all-gather.2.cloned.1.call-done = bf16[2,256,7168]{2,1,0:T(8,128)(2,1)} async-done(((bf16[2,64,7168]{2,1,0:T(8,128)(2,1)}), bf16[2,256,7168]{2,1,0:T(8,128)(2,1)}) %all-gather.2.cloned.1.call-update) | async-done | bytes 7340048 | tf_op jit(solution)/shard_map/all_gather | solution.py:108
  138.9 7.2 %fusion.34 = f32[2,256,256]{2,1,0:T(8,128)S(1)} fusion(bf16[2,256,7168]{2,1,0:T(8,128)(2,1)} %all-gather.2.cloned.1.call-done, bf16[2,7168,256]{2,1,0:T(8,128)(2,1)} %param.21), kind=kOutput, calls=%fused_computation.65 | convolution fusion | flops 1879048192 | bytes 15204352 | tf_op jit(solution)/shard_map/vmap()/dot_general | solution.py:51
  146.1 14.3 %convolution_convert_fusion = bf16[2,256,7168]{2,1,0:T(8,128)(2,1)} fusion(bf16[2,256,7168]{2,1,0:T(8,128)(2,1)} %param.23, bf16[2,256,7168]{2,1,0:T(8,128)(2,1)} %all-gather.2.cloned.1.call-done, bf16[2,7168,256]{2,1,0:T(8,128)(2,1)} %param.22, f32[2,256,256]{2,1,0:T(8,128)S(1)} %fusion.34), kind=kOutput, calls=%fused_computation.5 | convolution fusion | flops 3762552832 | bytes 29884416 | tf_op jit(solution)/shard_map/vmap()/dot_general | solution.py:54
  160.5 0.0 reduce-scatter.2.cloned.1.call-update
  160.5 73.6 %reduce-scatter.2.cloned.1.call-done = bf16[2,64,7168]{2,1,0:T(8,128)(2,1)} async-done(((bf16[2,256,7168]{2,1,0:T(8,128)(2,1)}), bf16[2,64,7168]{2,1,0:T(8,128)(2,1)}) %reduce-scatter.2.cloned.1.call-update) | async-done | bytes 1835024 | tf_op jit(solution)/shard_map/reduce_scatter | solution.py:111
  234.1 3.9 %convert_element_type.52 = bf16[2,32,2,7168]{3,2,1,0:T(2,128)(2,1)S(1)} reshape(bf16[2,64,7168]{2,1,0:T(8,128)(2,1)} %reduce-scatter.2.cloned.1.call-done) | data formatting | bytes 3670016 | tf_op jit(solution)/shard_map/convert_element_type | solution.py:115
  238.0 2.5 copy.27
  240.5 0.0 copy-start.5
  240.5 7.9 %all-to-all-start.2 = ((bf16[2,32,2,7168]{3,2,0,1:T(2,128)(2,1)}), bf16[2,32,2,7168]{3,2,0,1:T(2,128)(2,1)S(1)}, u32[]{:S(2)}, u32[]{:S(2)}) async-start(bf16[2,32,2,7168]{3,2,0,1:T(2,128)(2,1)} %copy.27), calls=%async_computation.3 | async-start | bytes 3670016 | tf_op jit(solution)/shard_map/all_to_all | solution.py:114
  248.4 0.0 copy-start.2
  248.4 0.0 copy-start.3
  248.5 0.0 copy-done.5
  248.5 0.1 iota_compare_fusion.1
  248.5 0.0 copy-done
  248.5 1.7 fusion.33
  250.2 0.0 copy-done.2
  250.2 0.0 copy-done.3
  250.2 0.3 fusion.5
  250.6 0.2 fusion.32
  250.8 1.7 convolution_convert_fusion.1
  252.5 21.5 %all-to-all-done.2 = bf16[2,32,2,7168]{3,2,0,1:T(2,128)(2,1)S(1)} async-done(((bf16[2,32,2,7168]{3,2,0,1:T(2,128)(2,1)}), bf16[2,32,2,7168]{3,2,0,1:T(2,128)(2,1)S(1)}, u32[]{:S(2)}, u32[]{:S(2)}) %all-to-all-start.2) | async-done | bytes 1835040 | tf_op jit(solution)/shard_map/all_to_all | solution.py:114
  273.9 2.5 copy.28
  276.4 4.1 %reshape.287 = bf16[128,7168]{1,0:T(8,128)(2,1)S(1)} reshape(bf16[2,32,2,7168]{3,2,1,0:T(2,128)(2,1)} %copy.28) | data formatting | bytes 3670016 | tf_op jit(solution)/shard_map/reshape | solution.py:121
  280.5 0.0 copy-start.4
  280.5 0.0 copy-start.1
  280.5 2.1 gather_fusion.1
  282.6 0.0 copy-done.4
  282.6 1.6 fusion.7
  284.2 0.0 copy-done.1
  284.2 0.7 fusion.19
  (8 shorter events, 0.1 us)
Async XLA Ops:
  7.2 241.4 %copy-start = (bf16[8,128,512]{2,1,0:T(8,128)(2,1)S(1)}, bf16[8,128,512]{2,1,0:T(8,128)(2,1)}, u32[]{:S(2)}) copy-start(bf16[8,128,512]{2,1,0:T(8,128)(2,1)} %param.14) | copy-start | bytes 3145732
  7.2 131.7 %all-gather.2.cloned.1.call-start = ((), (), s32[]{:S(2)}) async-start(), calls=%async_computation.4 | async-start | bytes 9175040 | tf_op jit(solution)/shard_map/all_gather | solution.py:108
  65.6 168.6 %reduce-scatter.2.cloned.1.call-start = ((), (), s32[]{:S(2)}) async-start(), calls=%async_computation.5 | async-start | bytes 9175040 | tf_op jit(solution)/shard_map/reduce_scatter | solution.py:111
  240.5 7.9 %copy-start.5 = (s32[8]{0:T(128)S(1)}, s32[8]{0:T(128)}, u32[]{:S(2)}) copy-start(s32[8]{0:T(128)} %param.16) | copy-start | bytes 100
  240.5 33.4 %all-to-all-start.2 = ((bf16[2,32,2,7168]{3,2,0,1:T(2,128)(2,1)}), bf16[2,32,2,7168]{3,2,0,1:T(2,128)(2,1)S(1)}, u32[]{:S(2)}, u32[]{:S(2)}) async-start(bf16[2,32,2,7168]{3,2,0,1:T(2,128)(2,1)} %copy.27), calls=%async_computation.3 | async-start | bytes 3670016 | tf_op jit(solution)/shard_map/all_to_all | solution.py:114
  248.4 1.8 copy-start.2
  248.4 1.8 copy-start.3
  280.5 2.1 copy-start.4
  280.5 3.6 %copy-start.1 = (bf16[8,7168]{1,0:T(8,128)(2,1)S(1)}, bf16[8,7168]{1,0:T(8,128)(2,1)}, u32[]{:S(2)}) copy-start(bf16[8,7168]{1,0:T(8,128)(2,1)} %param.17) | copy-start | bytes 344068
Sparse Core Ops, SparseCore 0:
  65.7 73.1 all-gather.1
  160.6 73.4 reduce-scatter.1
where the time goes:
time: 292 us
  waiting for transfers between devices  168 us (58%)
  blocking collectives  38.4 us (13%)
  local copies, waits for them, and re-layouts  29.2 us (10%)
  matrix products  26.8 us (9%)
  between operations  14.3 us (5%)
  starting transfers between devices  8.16 us (3%)
  other arithmetic  6.57 us (2%)
    reduce_scatter x1, waiting for transfers between devices, per_device(): lax.psum_scatter(partials.astype(jnp.float32).astype(jnp.bfloat16), 'rep'...  73.6 us
    all_gather x1, waiting for transfers between devices, per_device(): everyone = lax.all_gather(incoming, 'rep', axis=1, tiled=True)  73.1 us
    all_to_all x2, blocking collectives, moved_by_axis(): result = lax.all_to_all(result, axes[k], k, k, tiled=True)  38.4 us
    all_to_all x1, waiting for transfers between devices, per_device(): lax.all_to_all(summed.reshape(local_count, ep_count, capacity, feature_di...  21.5 us
    dot_general x1, matrix products, expert_block(): jnp.dot(hidden, down_part, preferred_element_type=jnp.float32)  14.3 us
    all_to_all x1, starting transfers between devices, per_device(): lax.all_to_all(summed.reshape(local_count, ep_count, capacity, feature_di...  7.9 us
    dot_general x1, matrix products, expert_block(): gate_act = jnp.dot(tokens_in, gate_part, preferred_element_type=jnp.float32)  7.22 us
    convert_element_type x2, local copies, waits for them, and re-layouts, per_device(): summed.reshape(local_count, ep_count, capacity, feature_dim)  6.39 us
  transfers between devices with their start and end apart: 3, of which 3 were waited for; matrix products, arithmetic and copies ran while one was open for 1% of the time, Pallas kernels for 0%

commit v1 on v0

--- a/solution.py
+++ b/solution.py
@@ -105,7 +105,9 @@
     attn_latent = jnp.einsum(
         "iht,itl->ihl", attn_weights, cache_latent, preferred_element_type=jnp.float32
     ).astype(jnp.bfloat16)
-    everyone = lax.all_gather(incoming, "rep", axis=1, tiled=True)
+    everyone = jnp.concatenate(
+        lax.all_to_all(jnp.stack([incoming] * lax.axis_size("rep")), "rep", 0, 0), axis=1
+    )
     partials = jax.vmap(expert_block)(everyone, w_gate, w_up, w_down)
     partials = lax.optimization_barrier(partials)
     summed = lax.psum_scatter(

time: 292 us -> 307 us (1.051)
  blocking collectives: 38.4 us -> 123 us
  waiting for transfers between devices: 168 us -> 92.1 us
  local copies, waits for them, and re-layouts: 29.2 us -> 35.4 us
    all_to_all x0 -> x1, blocking collectives: none -> 84.3 us  [per_device(): lax.all_to_all(jnp.stack([incoming] * lax.axis_size('rep')), 'rep', 0, 0)]
    all_gather x1 -> x0, waiting for transfers between devices: 73.1 us -> none  [per_device(): everyone = lax.all_gather(incoming, 'rep', axis=1, tiled=True)]
    reshape x0 -> x1, local copies, waits for them, and re-layouts: none -> 3.5 us  [per_device(): jnp.concatenate(lax.all_to_all(jnp.stack([incoming] * lax.axis_size('rep'...]
  transfers between devices with their start and end apart: 3 -> 2, of which waited for: 3 -> 2; matrix products, arithmetic and copies ran while one was open for 1% -> 2% of each run, Pallas kernels for 0% -> 0%
where the time goes in v1:
time: 307 us; the launch traced here: 306 us
  blocking collectives  123 us (40%)
  waiting for transfers between devices  92.1 us (30%)
  local copies, waits for them, and re-layouts  35.4 us (12%)
  matrix products  27.6 us (9%)
  between operations  14.3 us (5%)
  starting transfers between devices  7.8 us (3%)
  other arithmetic  6.57 us (2%)
    all_to_all x1, blocking collectives, per_device(): lax.all_to_all(jnp.stack([incoming] * lax.axis_size('rep')), 'rep', 0, 0)  84.3 us
    reduce_scatter x1, waiting for transfers between devices, per_device(): lax.psum_scatter(partials.astype(jnp.float32).astype(jnp.bfloat16), 'rep'...  71.4 us
    all_to_all x2, blocking collectives, moved_by_axis(): result = lax.all_to_all(result, axes[k], k, k, tiled=True)  38.4 us
    all_to_all x1, waiting for transfers between devices, per_device(): lax.all_to_all(summed.reshape(local_count, ep_count, capacity, feature_di...  20.6 us
    dot_general x1, matrix products, expert_block(): jnp.dot(hidden, down_part, preferred_element_type=jnp.float32)  14.3 us
    all_to_all x1, starting transfers between devices, per_device(): lax.all_to_all(summed.reshape(local_count, ep_count, capacity, feature_di...  7.76 us
    dot_general x1, matrix products, expert_block(): gate_act = jnp.dot(tokens_in, gate_part, preferred_element_type=jnp.float32)  7.22 us
    convert_element_type x2, local copies, waits for them, and re-layouts, per_device(): summed.reshape(local_count, ep_count, capacity, feature_dim)  6.39 us
  transfers between devices with their start and end apart: 2, of which 2 were waited for; matrix products, arithmetic and copies ran while one was open for 2% of the time, Pallas kernels for 0%

profile of v1, /device:TPU:1, one launch (start us, length us, event | category | flops | bytes accessed | tf_op | source)
XLA Modules:
  0.0 306.5 jit_solution(13840302822940996875)
XLA Ops:
  7.2 0.0 copy-start
  7.2 0.0 reduce-scatter.2.cloned.1.call-start
  7.2 0.8 eq.29
  8.1 0.8 reshape.292
  8.8 0.1 fusion.20
  8.9 0.1 reduce_window_sum.11
  9.0 0.2 select_reduce_fusion
  9.2 0.8 scatter_custom_fusion
  10.0 1.1 fusion.16
  11.1 1.0 fusion.18
  12.1 1.7 gather_fusion
  13.8 1.7 gather.9
  15.5 1.0 scatter_custom_fusion.1
  16.5 0.1 mul.87
  16.7 3.1 %copy_multiply_fusion = bf16[2,32,1,2,7168]{4,3,0,1,2:T(2,128)(2,1)S(1)} fusion(bf16[2,32,1,2,7168]{4,3,1,0,2:T(2,128)(2,1)} %gather.9, bf16[2,32,2]{2,0,1:T(2,128)(2,1)S(1)} %copy.31), kind=kLoop, calls=%fused_computation.6 | loop fusion | flops 917504 | bytes 3670272 | tf_op jit(solution)/shard_map/mul | solution.py:47
  19.8 1.3 copy.33
  21.1 6.2 %all_to_all.20 = bf16[16,2,2,1,2,7168]{5,4,0,2,3,1:T(2,128)(2,1)S(1)} all-to-all(bf16[16,2,2,1,2,7168]{5,4,0,2,3,1:T(2,128)(2,1)S(1)} %copy.33), channel_id=1, replica_groups=mesh['rep'=4,'ep_0'=4,'ep_1'=4,'ep_2'=2] {'ep_2'}, dimensions={1} | all-to-all | bytes 3670016 | tf_op jit(solution)/shard_map/all_to_all | solution.py:28
  27.3 1.7 copy.34
  29.0 32.2 %all_to_all.21 = bf16[16,2,2,1,2,7168]{5,4,1,2,3,0:T(2,128)(2,1)S(1)} all-to-all(bf16[16,2,2,1,2,7168]{5,4,1,2,3,0:T(2,128)(2,1)S(1)} %copy.34), channel_id=1, replica_groups=mesh['rep'=4,'ep_0'=4,'ep_1'=4,'ep_2'=2] {'ep_0','ep_1'}, dimensions={0} | all-to-all | bytes 3670016 | tf_op jit(solution)/shard_map/all_to_all | solution.py:28
  61.2 1.3 copy.35
  62.5 1.4 copy.36
  64.0 0.4 copy.37
  64.3 3.9 %stack.3 = bf16[4,2,64,7168]{3,2,1,0:T(8,128)(2,1)} broadcast(bf16[2,64,7168]{2,1,0:T(8,128)(2,1)S(1)} %copy.37), dimensions={1,2,3} | broadcast | bytes 9175040 | tf_op jit(solution)/shard_map/stack | solution.py:109
  68.2 84.3 %all_to_all.22 = bf16[4,2,64,7168]{3,2,1,0:T(8,128)(2,1)S(1)} all-to-all(bf16[4,2,64,7168]{3,2,1,0:T(8,128)(2,1)} %stack.3), channel_id=1, replica_groups=mesh['rep'=4,'ep_0'=4,'ep_1'=4,'ep_2'=2] {'rep'}, dimensions={0} | all-to-all | bytes 14680064 | tf_op jit(solution)/shard_map/all_to_all | solution.py:109
  152.5 3.5 %copy.38 = bf16[2,4,64,7168]{3,2,1,0:T(8,128)(2,1)} copy(bf16[2,4,64,7168]{3,2,0,1:T(8,128)(2,1)S(1)} %bitcast.33) | data formatting | bytes 14680064 | tf_op jit(solution)/shard_map/reshape | solution.py:108
  156.0 7.2 %fusion.34 = f32[2,256,256]{2,1,0:T(8,128)S(1)} fusion(bf16[2,256,7168]{2,1,0:T(8,128)(2,1)} %bitcast.34, bf16[2,7168,256]{2,1,0:T(8,128)(2,1)} %param.21), kind=kOutput, calls=%fused_computation.65 | convolution fusion | flops 1879048192 | bytes 15204352 | tf_op jit(solution)/shard_map/vmap()/dot_general | solution.py:51
  163.2 14.3 %convolution_convert_fusion = bf16[2,256,7168]{2,1,0:T(8,128)(2,1)} fusion(bf16[2,256,7168]{2,1,0:T(8,128)(2,1)} %param.23, bf16[2,256,7168]{2,1,0:T(8,128)(2,1)} %bitcast.35, bf16[2,7168,256]{2,1,0:T(8,128)(2,1)} %param.22, f32[2,256,256]{2,1,0:T(8,128)S(1)} %fusion.34), kind=kOutput, calls=%fused_computation.5 | convolution fusion | flops 3762552832 | bytes 29884416 | tf_op jit(solution)/shard_map/vmap()/dot_general | solution.py:54
  177.5 0.0 reduce-scatter.2.cloned.1.call-update
  177.6 0.0 copy-start.4
  177.6 0.0 copy-start.2
  177.6 71.4 %reduce-scatter.2.cloned.1.call-done = bf16[2,64,7168]{2,1,0:T(8,128)(2,1)} async-done(((bf16[2,256,7168]{2,1,0:T(8,128)(2,1)}), bf16[2,64,7168]{2,1,0:T(8,128)(2,1)}) %reduce-scatter.2.cloned.1.call-update) | async-done | bytes 1835024 | tf_op jit(solution)/shard_map/reduce_scatter | solution.py:113
  249.0 3.9 %convert_element_type.52 = bf16[2,32,2,7168]{3,2,1,0:T(2,128)(2,1)S(1)} reshape(bf16[2,64,7168]{2,1,0:T(8,128)(2,1)} %reduce-scatter.2.cloned.1.call-done) | data formatting | bytes 3670016 | tf_op jit(solution)/shard_map/convert_element_type | solution.py:117
  252.9 2.5 copy.39
  255.4 7.8 %all-to-all-start.3 = ((bf16[2,32,2,7168]{3,2,0,1:T(2,128)(2,1)}), bf16[2,32,2,7168]{3,2,0,1:T(2,128)(2,1)S(1)}, u32[]{:S(2)}, u32[]{:S(2)}) async-start(bf16[2,32,2,7168]{3,2,0,1:T(2,128)(2,1)} %copy.39), calls=%async_computation.4 | async-start | bytes 3670016 | tf_op jit(solution)/shard_map/all_to_all | solution.py:116
  263.2 0.0 copy-done.4
  263.2 0.1 iota_compare_fusion.1
  263.3 0.0 copy-done
  263.3 1.6 fusion.33
  264.9 0.0 copy-done.2
  265.0 1.2 fusion.5
  266.2 0.2 fusion.32
  266.4 1.7 convolution_convert_fusion.1
  268.1 0.0 copy-start.3
  268.1 20.6 %all-to-all-done.3 = bf16[2,32,2,7168]{3,2,0,1:T(2,128)(2,1)S(1)} async-done(((bf16[2,32,2,7168]{3,2,0,1:T(2,128)(2,1)}), bf16[2,32,2,7168]{3,2,0,1:T(2,128)(2,1)S(1)}, u32[]{:S(2)}, u32[]{:S(2)}) %all-to-all-start.3) | async-done | bytes 1835040 | tf_op jit(solution)/shard_map/all_to_all | solution.py:116
  288.7 2.5 copy.40
  291.2 0.0 copy-start.1
  291.2 4.1 %reshape.297 = bf16[128,7168]{1,0:T(8,128)(2,1)S(1)} reshape(bf16[2,32,2,7168]{3,2,1,0:T(2,128)(2,1)} %copy.40) | data formatting | bytes 3670016 | tf_op jit(solution)/shard_map/reshape | solution.py:123
  295.3 2.1 gather_fusion.1
  297.4 0.0 copy-done.3
  297.4 1.6 fusion.7
  298.9 0.0 copy-done.1
  298.9 0.7 fusion.19
  (8 shorter events, 0.1 us)
Async XLA Ops:
  7.2 256.1 %copy-start = (bf16[8,128,512]{2,1,0:T(8,128)(2,1)S(1)}, bf16[8,128,512]{2,1,0:T(8,128)(2,1)}, u32[]{:S(2)}) copy-start(bf16[8,128,512]{2,1,0:T(8,128)(2,1)} %param.14) | copy-start | bytes 3145732
  7.2 241.8 %reduce-scatter.2.cloned.1.call-start = ((), (), s32[]{:S(2)}) async-start(), calls=%async_computation.5 | async-start | bytes 9175040 | tf_op jit(solution)/shard_map/reduce_scatter | solution.py:113
  177.6 85.7 %copy-start.4 = (s32[8]{0:T(128)S(1)}, s32[8]{0:T(128)}, u32[]{:S(2)}) copy-start(s32[8]{0:T(128)} %param.16) | copy-start | bytes 100
  177.6 87.4 %copy-start.2 = (bf16[8,128,64]{1,2,0:T(8,128)(2,1)S(1)}, bf16[8,128,64]{1,2,0:T(8,128)(2,1)}, u32[]{:S(2)}) copy-start(bf16[8,128,64]{1,2,0:T(8,128)(2,1)} %param.13) | copy-start | bytes 393220
  255.4 33.3 %all-to-all-start.3 = ((bf16[2,32,2,7168]{3,2,0,1:T(2,128)(2,1)}), bf16[2,32,2,7168]{3,2,0,1:T(2,128)(2,1)S(1)}, u32[]{:S(2)}, u32[]{:S(2)}) async-start(bf16[2,32,2,7168]{3,2,0,1:T(2,128)(2,1)} %copy.39), calls=%async_computation.4 | async-start | bytes 3670016 | tf_op jit(solution)/shard_map/all_to_all | solution.py:116
  268.1 29.3 %copy-start.3 = (bf16[8,8]{1,0:T(8,128)(2,1)S(1)}, bf16[8,8]{1,0:T(8,128)(2,1)}, u32[]{:S(2)}) copy-start(bf16[8,8]{1,0:T(8,128)(2,1)} %param.20) | copy-start | bytes 388
  291.2 7.7 %copy-start.1 = (bf16[8,7168]{1,0:T(8,128)(2,1)S(1)}, bf16[8,7168]{1,0:T(8,128)(2,1)}, u32[]{:S(2)}) copy-start(bf16[8,7168]{1,0:T(8,128)(2,1)} %param.17) | copy-start | bytes 344068
Sparse Core Ops, SparseCore 0:
  177.7 71.3 reduce-scatter.1
